TPU v7x, 32 devices: a whole 2x2x4 slice. The times are simulated.
32 devices in a mesh: groups: 2 (over y), seq: 16 (over z, x, core).
Axes of the slice: x: 2, y: 2, z: 4, core: 2. Of those that a mesh axis runs over, the one named last changes fastest.
Arguments:
- queries: bfloat16 [12288, 2048], P(('groups', 'seq')), parts along dimension 0, may hold values from -6 to 6
- key_vectors: bfloat16 [12288, 2048], P(('groups', 'seq')), parts along dimension 0, may hold values from -6 to 6
- value_vectors: bfloat16 [12288, 2048], P(('groups', 'seq')), parts along dimension 0, may hold values from -6 to 6
- out_cotangent: bfloat16 [12288, 2048], P(('groups', 'seq')), parts along dimension 0, may hold values from -6 to 6
- norm_gain: float32 [2048], replicated, may hold values from 0.1 to 1.9
Outputs:
- query_grad: bfloat16 [12288, 2048], P(('groups', 'seq')), parts along dimension 0
- key_grad: bfloat16 [12288, 2048], P(('groups', 'seq')), parts along dimension 0
- value_grad: bfloat16 [12288, 2048], P(('groups', 'seq')), parts along dimension 0
- gain_grad: float32 [4096], P('groups'), parts along dimension 0
There are 2 independent parts, one for each index of `groups`. A program takes and returns all parts, laid end to end along the dimension named above; an argument that names none is the same for every part. Nothing has to cross between parts.
All inputs are finite; a program needn't handle non-finite values.
Results may differ from a plain program's by a relative error of at most 0.011.
Values may be sent and summed in bfloat16 or wider, within the bound.
No kernel may reach another device: no remote copies, remote signals or barrier semaphores. Data moves between devices by JAX's collectives and lax.ppermute only.
A program may use at most 128 MiB of HBM per device.

v0:
```python
import jax
import jax.numpy as jnp
from jax import lax
from jax.sharding import PartitionSpec as P

HEADS = 16
HEAD = 128
norm_eps = 1e-05


def shifted(value, axis, steps):
    count = lax.axis_size(axis)
    first, last = (max(0, -steps), min(count, count - steps))
    return lax.ppermute(value, axis, [(source, source + steps) for source in range(first, last)])


def feature(x):
    return jnp.where(x > 0, x + 1.0, jnp.exp(jnp.minimum(x, 0.0)))


def slope(x):
    return jnp.where(x > 0, 1.0, jnp.exp(jnp.minimum(x, 0.0)))


def on_device(queries, key_vectors, value_vectors, out_cotangent, norm_gain):
    length = queries.shape[0]
    shards = lax.axis_size("seq")
    rounds = (shards - 1).bit_length()
    query_raw = queries.reshape(length, HEADS, HEAD)
    key_raw = key_vectors.reshape(length, HEADS, HEAD)
    value_rows = value_vectors.reshape(length, HEADS, HEAD)
    cotan = out_cotangent.reshape(length, HEADS, HEAD).astype(jnp.float32)
    query_map = feature(query_raw.astype(jnp.float32)).astype(jnp.bfloat16)
    key_map = feature(key_raw.astype(jnp.float32)).astype(jnp.bfloat16)
    own_state = jnp.einsum("thd,the->hde", key_map, value_rows, preferred_element_type=jnp.float32)
    running = own_state
    for level in range(rounds):
        running = running + shifted(running, "seq", 1 << level)
    state_low = (running - own_state).astype(jnp.bfloat16)
    causal = jnp.tril(jnp.ones((length, length), dtype=bool))[None]
    scores = jnp.einsum("thd,shd->hts", query_map, key_map, preferred_element_type=jnp.float32)
    weights = jnp.where(causal, scores, 0.0).astype(jnp.bfloat16)
    mixed = jnp.einsum("hts,she->the", weights, value_rows, preferred_element_type=jnp.float32)
    mixed = mixed + jnp.einsum(
        "thd,hde->the", query_map, state_low, preferred_element_type=jnp.float32
    )
    rms = jnp.sqrt(jnp.mean(mixed * mixed, axis=-1, keepdims=True) + norm_eps)
    normed = mixed / rms
    gain_part = jnp.sum(cotan * normed, axis=0)
    scaled = cotan * norm_gain.reshape(HEADS, HEAD)
    grad_mixed = (
        (scaled - normed * jnp.mean(scaled * normed, axis=-1, keepdims=True)) / rms
    ).astype(jnp.bfloat16)
    query_state = jnp.einsum(
        "thd,the->hde", query_map, grad_mixed, preferred_element_type=jnp.float32
    )
    later = query_state
    for level in range(rounds):
        later = later + shifted(later, "seq", -(1 << level))
    back_low = (later - query_state).astype(jnp.bfloat16)
    gain_total = lax.psum(gain_part, "seq")
    d_scores = jnp.einsum(
        "the,she->hts", grad_mixed, value_rows, preferred_element_type=jnp.float32
    )
    d_weights = jnp.where(causal, d_scores, 0.0).astype(jnp.bfloat16)
    d_query = jnp.einsum("hts,shd->thd", d_weights, key_map, preferred_element_type=jnp.float32)
    d_query = d_query + jnp.einsum(
        "the,hde->thd", grad_mixed, state_low, preferred_element_type=jnp.float32
    )
    d_key = jnp.einsum("hts,thd->shd", d_weights, query_map, preferred_element_type=jnp.float32)
    d_key = d_key + jnp.einsum(
        "the,hde->thd", value_rows, back_low, preferred_element_type=jnp.float32
    )
    d_value = jnp.einsum("hts,the->she", weights, grad_mixed, preferred_element_type=jnp.float32)
    d_value = d_value + jnp.einsum(
        "thd,hde->the", key_map, back_low, preferred_element_type=jnp.float32
    )
    query_grad = (d_query * slope(query_raw.astype(jnp.float32))).astype(jnp.bfloat16)
    key_grad = (d_key * slope(key_raw.astype(jnp.float32))).astype(jnp.bfloat16)
    value_grad = d_value.astype(jnp.bfloat16)
    flat = (length, HEADS * HEAD)
    return (
        query_grad.reshape(flat),
        key_grad.reshape(flat),
        value_grad.reshape(flat),
        gain_total.reshape(HEADS * HEAD),
    )


def solution(mesh):
    placed = (
        P(("groups", "seq"), None),
        P(("groups", "seq"), None),
        P(("groups", "seq"), None),
        P(("groups", "seq"), None),
        P(),
    )
    return jax.shard_map(
        on_device,
        mesh=mesh,
        in_specs=placed,
        out_specs=(
            P(("groups", "seq"), None),
            P(("groups", "seq"), None),
            P(("groups", "seq"), None),
            P("groups"),
        ),
        check_vma=False,
    )
```

profile of v0, /device:TPU:16, one launch (start us, length us, event | category | flops | bytes accessed | tf_op | source)
XLA Modules:
  0.0 292.3 jit_solution(8299461528966683161)
XLA Ops:
  0.6 0.0 copy-start
  0.6 4.7 %fusion.3 = (f32[384,2048]{1,0:T(8,128)}, bf16[48,16,8,128]{3,2,1,0:T(8,128)(2,1)}, bf16[48,8,16,128]{3,1,2,0:T(8,128)(2,1)S(1)}) fusion(bf16[384,2048]{1,0:T(8,128)(2,1)} %param.6), kind=kLoop, calls=%fused_computation.11 | loop fusion | flops 5505024 | bytes 7864320 | tf_op jit(solution)/shard_map/jit(_where)/select_n | solution.py:22
  5.3 1.6 copy.40
  6.9 2.1 copy.19
  9.0 0.0 copy-done
  9.0 0.0 copy-start.6
  9.0 0.6 fusion.14
  9.6 1.9 collective-permute-start
  11.5 15.1 %collective-permute-done = f32[16,128,128]{2,1,0:T(8,128)S(1)} collective-permute-done((f32[16,128,128]{2,1,0:T(8,128)S(1)}, f32[16,128,128]{2,1,0:T(8,128)S(1)}, u32[]{:S(2)}, u32[]{:S(2)}) %collective-permute-start) | collective-permute-done | bytes 1048608 | tf_op jit(solution)/shard_map/ppermute | solution.py:14
  26.6 0.2 add.66
  26.8 2.5 collective-permute-start.1
  29.3 23.6 %collective-permute-done.1 = f32[16,128,128]{2,1,0:T(8,128)S(1)} collective-permute-done((f32[16,128,128]{2,1,0:T(8,128)S(1)}, f32[16,128,128]{2,1,0:T(8,128)S(1)}, u32[]{:S(2)}, u32[]{:S(2)}) %collective-permute-start.1) | collective-permute-done | bytes 1048608 | tf_op jit(solution)/shard_map/ppermute | solution.py:14
  52.9 0.1 add.67
  53.0 0.0 copy-start.17
  53.0 3.6 %collective-permute-start.2 = (f32[16,128,128]{2,1,0:T(8,128)S(1)}, f32[16,128,128]{2,1,0:T(8,128)S(1)}, u32[]{:S(2)}, u32[]{:S(2)}) collective-permute-start(f32[16,128,128]{2,1,0:T(8,128)S(1)} %add.67), channel_id=1, source_target_pairs={{0,4},{1,5},{2,6},{3,7},{4,8},{5,9},{6,10},{7,11},{8,12},{9,13},{1... | collective-permute-start | bytes 3145736 | tf_op jit(solution)/shard_map/ppermute | solution.py:14
  56.7 20.8 %collective-permute-done.2 = f32[16,128,128]{2,1,0:T(8,128)S(1)} collective-permute-done((f32[16,128,128]{2,1,0:T(8,128)S(1)}, f32[16,128,128]{2,1,0:T(8,128)S(1)}, u32[]{:S(2)}, u32[]{:S(2)}) %collective-permute-start.2) | collective-permute-done | bytes 1048608 | tf_op jit(solution)/shard_map/ppermute | solution.py:14
  77.4 1.1 add.68
  78.6 1.4 collective-permute-start.3
  80.0 3.1 %fusion.5 = (bf16[384,2048]{1,0:T(8,128)(2,1)}, f32[384,2048]{1,0:T(8,128)}) fusion(bf16[384,2048]{1,0:T(8,128)(2,1)S(1)} %copy-done.17), kind=kLoop, calls=%fused_computation.13 | loop fusion | flops 5505024 | bytes 6291456 | tf_op jit(solution)/shard_map/convert.1
  83.0 2.1 copy.9
  85.2 1.9 copy.37
  87.1 3.1 %select_convert_fusion.1 = bf16[16,384,384]{2,1,0:T(8,128)(2,1)S(1)} fusion(pred[384,384]{1,0:T(8,128)(4,1)S(1)} %iota_compare_fusion, bf16[384,16,128]{0,2,1:T(8,128)(2,1)S(1)} %bitcast.76, bf16[48,16,8,128]{3,2,1,0:T(8,128)(2,1)} %get-tuple-element.11), kind=kOutput, calls=%fused_computation.1 | convolution fusion | flops 608698368 | bytes 8011776 | tf_op jit(solution)/shard_map/thd,shd->hts/dot_general | solution.py:41
  90.2 1.6 fusion.10
  91.9 0.5 copy-done.4
  92.3 11.0 %collective-permute-done.3 = f32[16,128,128]{2,1,0:T(8,128)} collective-permute-done((f32[16,128,128]{2,1,0:T(8,128)}, f32[16,128,128]{2,1,0:T(8,128)}, u32[]{:S(2)}, u32[]{:S(2)}) %collective-permute-start.3) | collective-permute-done | bytes 1048608 | tf_op jit(solution)/shard_map/ppermute | solution.py:14
  103.3 1.8 subtract_convert_fusion.1
  105.1 0.0 copy-start.19
  105.1 0.7 multiply_reduce_fusion.2
  105.9 0.0 copy-done.14
  105.9 1.3 copy-done.1
  107.2 1.3 multiply_reduce_fusion
  108.5 0.8 divide_convert_fusion
  109.3 0.0 copy-start.2
  109.3 0.8 fusion.28
  110.1 23.0 %collective-permute-start.4 = (f32[16,128,128]{2,1,0:T(8,128)S(1)}, f32[16,128,128]{2,1,0:T(8,128)S(1)}, u32[]{:S(2)}, u32[]{:S(2)}) collective-permute-start(f32[16,128,128]{2,1,0:T(8,128)S(1)} %fusion.28), channel_id=1, source_target_pairs={{1,0},{2,1},{3,2},{4,3},{5,4},{6,5},{7,6},{8,7},{9,8},{10,9},{11,1... | collective-permute-start | bytes 3145736 | tf_op jit(solution)/shard_map/ppermute | solution.py:14
  133.1 12.3 %collective-permute-done.4 = f32[16,128,128]{2,1,0:T(8,128)S(1)} collective-permute-done((f32[16,128,128]{2,1,0:T(8,128)S(1)}, f32[16,128,128]{2,1,0:T(8,128)S(1)}, u32[]{:S(2)}, u32[]{:S(2)}) %collective-permute-start.4) | collective-permute-done | bytes 1048608 | tf_op jit(solution)/shard_map/ppermute | solution.py:14
  145.4 0.2 add.75
  145.6 3.8 %collective-permute-start.5 = (f32[16,128,128]{2,1,0:T(8,128)S(1)}, f32[16,128,128]{2,1,0:T(8,128)S(1)}, u32[]{:S(2)}, u32[]{:S(2)}) collective-permute-start(f32[16,128,128]{2,1,0:T(8,128)S(1)} %add.75), channel_id=1, source_target_pairs={{2,0},{3,1},{4,2},{5,3},{6,4},{7,5},{8,6},{9,7},{10,8},{11,9},{12,... | collective-permute-start | bytes 3145736 | tf_op jit(solution)/shard_map/ppermute | solution.py:14
  149.4 23.2 %collective-permute-done.5 = f32[16,128,128]{2,1,0:T(8,128)S(1)} collective-permute-done((f32[16,128,128]{2,1,0:T(8,128)S(1)}, f32[16,128,128]{2,1,0:T(8,128)S(1)}, u32[]{:S(2)}, u32[]{:S(2)}) %collective-permute-start.5) | collective-permute-done | bytes 1048608 | tf_op jit(solution)/shard_map/ppermute | solution.py:14
  172.7 1.1 add.76
  173.7 0.0 copy-done.9
  173.7 2.9 collective-permute-start.6
  176.6 3.5 %copy.21 = f32[384,2048]{0,1:T(8,128)} copy(f32[384,2048]{1,0:T(8,128)} %get-tuple-element.14) | data formatting | bytes 6291456 | tf_op jit(solution)/shard_map/jit(_where)/select_n | solution.py:22
  180.1 3.5 %copy.26 = f32[384,2048]{0,1:T(8,128)} copy(f32[384,2048]{1,0:T(8,128)} %get-tuple-element.10) | data formatting | bytes 6291456 | tf_op jit(solution)/shard_map/jit(_where)/select_n | solution.py:22
  183.7 3.2 %select_convert_fusion = bf16[16,384,384]{2,1,0:T(8,128)(2,1)S(1)} fusion(pred[384,384]{1,0:T(8,128)(4,1)S(1)} %iota_compare_fusion, bf16[384,16,128]{0,2,1:T(8,128)(2,1)} %copy-done.2, bf16[384,2048]{1,0:T(8,128)(2,1)S(1)} %copy-done), kind=kOutput, calls=%fused_computation | convolution fusion | flops 608698368 | bytes 8011776 | tf_op jit(solution)/shard_map/the,she->hts/dot_general | solution.py:62
  186.9 1.6 fusion.26
  188.5 0.8 copy-done.5
  189.3 12.7 %collective-permute-done.6 = f32[16,128,128]{2,1,0:T(8,128)} collective-permute-done((f32[16,128,128]{2,1,0:T(8,128)}, f32[16,128,128]{2,1,0:T(8,128)}, u32[]{:S(2)}, u32[]{:S(2)}) %collective-permute-start.6) | collective-permute-done | bytes 1048608 | tf_op jit(solution)/shard_map/ppermute | solution.py:14
  202.0 2.6 add.77
  204.6 3.1 %collective-permute-start.7 = (f32[16,128,128]{2,1,0:T(8,128)}, f32[16,128,128]{2,1,0:T(8,128)}, u32[]{:S(2)}, u32[]{:S(2)}) collective-permute-start(f32[16,128,128]{2,1,0:T(8,128)} %add.77), channel_id=1, source_target_pairs={{8,0},{9,1},{10,2},{11,3},{12,4},{13,5},{14,6},{15,7},{24,16},{25,... | collective-permute-start | bytes 3145736 | tf_op jit(solution)/shard_map/ppermute | solution.py:14
  207.7 0.0 copy-done.15
  207.7 2.0 fusion.9
  209.6 2.6 copy.29
  212.2 60.8 %psum.7 = f32[2048]{0:T(1024)} all-reduce(f32[2048]{0:T(1024)S(1)} %bitcast.88), channel_id=1, replica_groups=mesh['groups'=2,'seq'=16] {'seq'}, use_global_device_ids=true, to_apply=%region_3.4 | all-reduce | flops 2048 | bytes 16384 | tf_op jit(solution)/shard_map/psum | solution.py:61
  273.1 4.0 %fusion.29 = f32[16,128,384]{2,1,0:T(8,128)S(1)} fusion(bf16[384,16,128]{0,2,1:T(8,128)(2,1)} %copy-done.2, bf16[16,384,384]{2,1,0:T(8,128)(2,1)} %copy-done.4), kind=kOutput, calls=%fused_computation.51 | convolution fusion | flops 603979776 | bytes 9437184 | tf_op jit(solution)/shard_map/hts,the->she/dot_general | solution.py:74
  277.1 5.3 %fusion.27 = f32[16,128,384]{2,1,0:T(8,128)} fusion(bf16[384,16,128]{0,2,1:T(8,128)(2,1)S(1)} %bitcast.79, bf16[16,384,384]{2,1,0:T(8,128)(2,1)} %copy-done.5), kind=kOutput, calls=%fused_computation.49 | convolution fusion | flops 603979776 | bytes 9437184 | tf_op jit(solution)/shard_map/hts,thd->shd/dot_general | solution.py:70
  282.4 0.0 collective-permute-done.7
  282.4 0.0 copy-done.10
  282.4 1.9 subtract_convert_fusion
  284.3 0.1 copy-done.13
  284.5 0.8 add_convert_fusion
  285.3 1.6 copy.31
  286.9 3.8 %fusion.8 = bf16[384,16,128]{0,2,1:T(8,128)(2,1)S(1)} fusion(f32[384,16,128]{0,2,1:T(8,128)} %bitcast.80, f32[16,128,384]{2,1,0:T(8,128)} %fusion.27, bf16[16,128,128]{2,1,0:T(8,128)(2,1)} %copy-done.16, bf16[384,2048]{1,0:T(8,128)(2,1)S(1)} %copy-done), kind=kOutput, calls=%fused_computation.17 | convolution fusion | flops 203685888 | bytes 9961472 | tf_op jit(solution)/shard_map/the,hde->thd/dot_general | solution.py:71
  290.7 1.6 copy.30
  (29 shorter events, 0.1 us)
Async XLA Ops:
  0.6 8.4 %copy-start = (bf16[384,2048]{1,0:T(8,128)(2,1)S(1)}, bf16[384,2048]{1,0:T(8,128)(2,1)}, u32[]{:S(2)}) copy-start(bf16[384,2048]{1,0:T(8,128)(2,1)} %param.7) | copy-start | bytes 4718596
  9.0 17.8 %copy-start.6 = (bf16[384,16,128]{0,2,1:T(8,128)(2,1)}, bf16[384,16,128]{0,2,1:T(8,128)(2,1)S(1)}, u32[]{:S(2)}) copy-start(bf16[384,16,128]{0,2,1:T(8,128)(2,1)S(1)} %copy.19) | copy-start | bytes 4718596
  9.6 43.4 %copy-start.11 = (f32[16,128,128]{2,1,0:T(8,128)}, f32[16,128,128]{2,1,0:T(8,128)S(1)}, u32[]{:S(2)}) copy-start(f32[16,128,128]{2,1,0:T(8,128)S(1)} %fusion.14) | copy-start | bytes 3145732
  9.6 17.0 %collective-permute-start = (f32[16,128,128]{2,1,0:T(8,128)S(1)}, f32[16,128,128]{2,1,0:T(8,128)S(1)}, u32[]{:S(2)}, u32[]{:S(2)}) collective-permute-start(f32[16,128,128]{2,1,0:T(8,128)S(1)} %fusion.14), channel_id=1, source_target_pairs={{0,1},{1,2},{2,3},{3,4},{4,5},{5,6},{6,7},{7,8},{8,9},{9,10},{10,1... | collective-permute-start | bytes 3145736 | tf_op jit(solution)/shard_map/ppermute | solution.py:14
  26.8 26.1 %collective-permute-start.1 = (f32[16,128,128]{2,1,0:T(8,128)S(1)}, f32[16,128,128]{2,1,0:T(8,128)S(1)}, u32[]{:S(2)}, u32[]{:S(2)}) collective-permute-start(f32[16,128,128]{2,1,0:T(8,128)S(1)} %add.66), channel_id=1, source_target_pairs={{0,2},{1,3},{2,4},{3,5},{4,6},{5,7},{6,8},{7,9},{8,10},{9,11},{10,... | collective-permute-start | bytes 3145736 | tf_op jit(solution)/shard_map/ppermute | solution.py:14
  53.0 27.0 %copy-start.17 = (bf16[384,2048]{1,0:T(8,128)(2,1)S(1)}, bf16[384,2048]{1,0:T(8,128)(2,1)}, u32[]{:S(2)}) copy-start(bf16[384,2048]{1,0:T(8,128)(2,1)} %param.5) | copy-start | bytes 4718596
  53.0 24.4 %collective-permute-start.2 = (f32[16,128,128]{2,1,0:T(8,128)S(1)}, f32[16,128,128]{2,1,0:T(8,128)S(1)}, u32[]{:S(2)}, u32[]{:S(2)}) collective-permute-start(f32[16,128,128]{2,1,0:T(8,128)S(1)} %add.67), channel_id=1, source_target_pairs={{0,4},{1,5},{2,6},{3,7},{4,8},{5,9},{6,10},{7,11},{8,12},{9,13},{1... | collective-permute-start | bytes 3145736 | tf_op jit(solution)/shard_map/ppermute | solution.py:14
  78.6 4.5 %copy-start.18 = (bf16[384,2048]{1,0:T(8,128)(2,1)S(1)}, bf16[384,2048]{1,0:T(8,128)(2,1)}, u32[]{:S(2)}) copy-start(bf16[384,2048]{1,0:T(8,128)(2,1)} %param.8) | copy-start | bytes 4718596
  78.6 24.8 %collective-permute-start.3 = (f32[16,128,128]{2,1,0:T(8,128)}, f32[16,128,128]{2,1,0:T(8,128)}, u32[]{:S(2)}, u32[]{:S(2)}) collective-permute-start(f32[16,128,128]{2,1,0:T(8,128)} %add.68), channel_id=1, source_target_pairs={{0,8},{1,9},{2,10},{3,11},{4,12},{5,13},{6,14},{7,15},{16,24},{17,... | collective-permute-start | bytes 3145736 | tf_op jit(solution)/shard_map/ppermute | solution.py:14
  90.2 2.1 copy-start.4
  90.2 13.1 %copy-start.12 = (f32[16,128,128]{2,1,0:T(8,128)S(1)}, f32[16,128,128]{2,1,0:T(8,128)}, u32[]{:S(2)}) copy-start(f32[16,128,128]{2,1,0:T(8,128)} %copy-done.11) | copy-start | bytes 3145732
  105.1 0.8 copy-start.14
  105.1 2.1 copy-start.1
  105.1 2.1 copy-start.19
  109.3 36.3 %copy-start.2 = (bf16[384,16,128]{0,2,1:T(8,128)(2,1)}, bf16[384,16,128]{0,2,1:T(8,128)(2,1)S(1)}, u32[]{:S(2)}) copy-start(bf16[384,16,128]{0,2,1:T(8,128)(2,1)S(1)} %divide_convert_fusion) | copy-start | bytes 4718596
  110.1 63.6 %copy-start.9 = (f32[16,128,128]{2,1,0:T(8,128)}, f32[16,128,128]{2,1,0:T(8,128)S(1)}, u32[]{:S(2)}) copy-start(f32[16,128,128]{2,1,0:T(8,128)S(1)} %fusion.28) | copy-start | bytes 3145732
  110.1 35.3 %collective-permute-start.4 = (f32[16,128,128]{2,1,0:T(8,128)S(1)}, f32[16,128,128]{2,1,0:T(8,128)S(1)}, u32[]{:S(2)}, u32[]{:S(2)}) collective-permute-start(f32[16,128,128]{2,1,0:T(8,128)S(1)} %fusion.28), channel_id=1, source_target_pairs={{1,0},{2,1},{3,2},{4,3},{5,4},{6,5},{7,6},{8,7},{9,8},{10,9},{11,1... | collective-permute-start | bytes 3145736 | tf_op jit(solution)/shard_map/ppermute | solution.py:14
  145.6 27.1 %collective-permute-start.5 = (f32[16,128,128]{2,1,0:T(8,128)S(1)}, f32[16,128,128]{2,1,0:T(8,128)S(1)}, u32[]{:S(2)}, u32[]{:S(2)}) collective-permute-start(f32[16,128,128]{2,1,0:T(8,128)S(1)} %add.75), channel_id=1, source_target_pairs={{2,0},{3,1},{4,2},{5,3},{6,4},{7,5},{8,6},{9,7},{10,8},{11,9},{12,... | collective-permute-start | bytes 3145736 | tf_op jit(solution)/shard_map/ppermute | solution.py:14
  173.7 28.2 %collective-permute-start.6 = (f32[16,128,128]{2,1,0:T(8,128)}, f32[16,128,128]{2,1,0:T(8,128)}, u32[]{:S(2)}, u32[]{:S(2)}) collective-permute-start(f32[16,128,128]{2,1,0:T(8,128)} %add.76), channel_id=1, source_target_pairs={{4,0},{5,1},{6,2},{7,3},{8,4},{9,5},{10,6},{11,7},{12,8},{13,9},{1... | collective-permute-start | bytes 3145736 | tf_op jit(solution)/shard_map/ppermute | solution.py:14
  183.7 3.2 %copy-start.7 = (bf16[384,16,128]{0,2,1:T(8,128)(2,1)S(1)}, bf16[384,16,128]{0,2,1:T(8,128)(2,1)}, u32[]{:S(2)}) copy-start(bf16[384,16,128]{0,2,1:T(8,128)(2,1)} %copy-done.6) | copy-start | bytes 4718596
  186.9 2.4 copy-start.5
  186.9 20.8 %copy-start.8 = (f32[384,2048]{0,1:T(8,128)S(1)}, f32[384,2048]{0,1:T(8,128)}, u32[]{:S(2)}) copy-start(f32[384,2048]{0,1:T(8,128)} %copy.21) | copy-start | bytes 9437188
  189.3 18.4 %copy-start.3 = (bf16[384,16,128]{0,2,1:T(8,128)(2,1)S(1)}, bf16[384,16,128]{0,2,1:T(8,128)(2,1)}, u32[]{:S(2)}) copy-start(bf16[384,16,128]{0,2,1:T(8,128)(2,1)} %copy-done.2) | copy-start | bytes 4718596
  189.3 18.4 %copy-start.15 = (bf16[16,128,128]{2,1,0:T(8,128)(2,1)S(1)}, bf16[16,128,128]{2,1,0:T(8,128)(2,1)}, u32[]{:S(2)}) copy-start(bf16[16,128,128]{2,1,0:T(8,128)(2,1)} %copy-done.14) | copy-start | bytes 1572868
  204.6 77.8 %collective-permute-start.7 = (f32[16,128,128]{2,1,0:T(8,128)}, f32[16,128,128]{2,1,0:T(8,128)}, u32[]{:S(2)}, u32[]{:S(2)}) collective-permute-start(f32[16,128,128]{2,1,0:T(8,128)} %add.77), channel_id=1, source_target_pairs={{8,0},{9,1},{10,2},{11,3},{12,4},{13,5},{14,6},{15,7},{24,16},{25,... | collective-permute-start | bytes 3145736 | tf_op jit(solution)/shard_map/ppermute | solution.py:14
  277.1 5.3 %copy-start.10 = (f32[16,128,128]{2,1,0:T(8,128)S(1)}, f32[16,128,128]{2,1,0:T(8,128)}, u32[]{:S(2)}) copy-start(f32[16,128,128]{2,1,0:T(8,128)} %copy-done.9) | copy-start | bytes 3145732
  282.4 2.0 copy-start.13
  284.5 0.8 copy-start.16
where the time goes:
time: 293 us; the launch traced here: 292 us
  waiting for transfers between devices  119 us (41%)
  blocking collectives  60.8 us (21%)
  starting transfers between devices  42.2 us (14%)
  matrix products  27.4 us (9%)
  local copies, waits for them, and re-layouts  23.4 us (8%)
  other arithmetic  18.8 us (6%)
    ppermute x8, waiting for transfers between devices, shifted(): lax.ppermute(value, axis, [(source, source + steps) for source in range(f...  119 us
    psum x1, blocking collectives, on_device(): gain_total = lax.psum(gain_part, 'seq')  60.8 us
    ppermute x8, starting transfers between devices, shifted(): lax.ppermute(value, axis, [(source, source + steps) for source in range(f...  42.2 us
    unnamed x44, local copies, waits for them, and re-layouts  10.2 us
    select_n x2, local copies, waits for them, and re-layouts, slope(): return jnp.where(x > 0, 1.0, jnp.exp(jnp.minimum(x, 0.0)))  7.07 us
  transfers between devices with their start and end apart: 8, of which 7 were waited for; matrix products, arithmetic and copies ran while one was open for 13% of the time, Pallas kernels for 0%

commit v1 on v0

--- a/solution.py
+++ b/solution.py
@@ -58,7 +58,11 @@
     for level in range(rounds):
         later = later + shifted(later, "seq", -(1 << level))
     back_low = (later - query_state).astype(jnp.bfloat16)
-    gain_total = lax.psum(gain_part, "seq")
+    gain_total = gain_part
+    for hop in (1, 2, 4, 8):
+        gain_total = gain_total + lax.ppermute(
+            gain_total, "seq", [(dev, dev ^ hop) for dev in range(16)]
+        )
     d_scores = jnp.einsum(
         "the,she->hts", grad_mixed, value_rows, preferred_element_type=jnp.float32
     )

time: 293 us -> 270 us (0.922); the launches traced: 292 us -> 265 us
  blocking collectives: 60.8 us -> 0 us
  waiting for transfers between devices: 119 us -> 151 us
  starting transfers between devices: 42.2 us -> 46.4 us
  matrix products: 27.4 us -> 23.9 us
    psum x1 -> x0, blocking collectives: 60.8 us -> none  [on_device(): gain_total = lax.psum(gain_part, 'seq')]
    ppermute x0 -> x4, waiting for transfers between devices: none -> 36.4 us  [on_device(): lax.ppermute(gain_total, 'seq', [(dev, dev ^ hop) for dev in range(16)])]
    ppermute x0 -> x4, starting transfers between devices: none -> 4.07 us  [on_device(): lax.ppermute(gain_total, 'seq', [(dev, dev ^ hop) for dev in range(16)])]
    ppermute x8, waiting for transfers between devices: 119 us -> 115 us  [shifted(): lax.ppermute(value, axis, [(source, source + steps) for source in range(f...]
    unnamed x44 -> x46, local copies, waits for them, and re-layouts: 10.2 us -> 9.42 us
  transfers between devices with their start and end apart: 8 -> 12, of which waited for: 7 -> 8; matrix products, arithmetic and copies ran while one was open for 13% -> 13% of each run, Pallas kernels for 0% -> 0%
where the time goes in v1:
time: 270 us; the launch traced here: 265 us
  waiting for transfers between devices  151 us (56%)
  starting transfers between devices  46.4 us (17%)
  matrix products  23.9 us (9%)
  local copies, waits for them, and re-layouts  22.8 us (8%)
  other arithmetic  19.5 us (7%)
    ppermute x8, waiting for transfers between devices, shifted(): lax.ppermute(value, axis, [(source, source + steps) for source in range(f...  115 us
    ppermute x8, starting transfers between devices, shifted(): lax.ppermute(value, axis, [(source, source + steps) for source in range(f...  42.3 us
    ppermute x4, waiting for transfers between devices, on_device(): lax.ppermute(gain_total, 'seq', [(dev, dev ^ hop) for dev in range(16)])  36.4 us
    unnamed x46, local copies, waits for them, and re-layouts  9.42 us
    select_n x2, local copies, waits for them, and re-layouts, slope(): return jnp.where(x > 0, 1.0, jnp.exp(jnp.minimum(x, 0.0)))  7.29 us
  transfers between devices with their start and end apart: 12, of which 8 were waited for; matrix products, arithmetic and copies ran while one was open for 13% of the time, Pallas kernels for 0%

profile of v1, /device:TPU:16, one launch (start us, length us, event | category | flops | bytes accessed | tf_op | source)
XLA Modules:
  0.0 264.7 jit_solution(8353340036778644456)
XLA Ops:
  0.6 0.0 copy-start
  0.6 4.9 %fusion.3 = (f32[384,2048]{1,0:T(8,128)}, bf16[48,16,8,128]{3,2,1,0:T(8,128)(2,1)}, bf16[48,8,16,128]{3,1,2,0:T(8,128)(2,1)S(1)}) fusion(bf16[384,2048]{1,0:T(8,128)(2,1)} %param.6), kind=kLoop, calls=%fused_computation.11 | loop fusion | flops 5505024 | bytes 7864320 | tf_op jit(solution)/shard_map/jit(_where)/select_n | solution.py:22
  5.5 1.6 copy.40
  7.1 2.1 copy.19
  9.2 0.0 copy-start.5
  9.3 0.6 fusion.14
  9.8 1.9 collective-permute-start
  11.8 15.1 %collective-permute-done = f32[16,128,128]{2,1,0:T(8,128)S(1)} collective-permute-done((f32[16,128,128]{2,1,0:T(8,128)S(1)}, f32[16,128,128]{2,1,0:T(8,128)S(1)}, u32[]{:S(2)}, u32[]{:S(2)}) %collective-permute-start) | collective-permute-done | bytes 1048608 | tf_op jit(solution)/shard_map/ppermute | solution.py:14
  26.9 0.1 add.76
  27.0 2.5 collective-permute-start.1
  29.5 23.6 %collective-permute-done.1 = f32[16,128,128]{2,1,0:T(8,128)S(1)} collective-permute-done((f32[16,128,128]{2,1,0:T(8,128)S(1)}, f32[16,128,128]{2,1,0:T(8,128)S(1)}, u32[]{:S(2)}, u32[]{:S(2)}) %collective-permute-start.1) | collective-permute-done | bytes 1048608 | tf_op jit(solution)/shard_map/ppermute | solution.py:14
  53.1 0.1 add.77
  53.2 0.0 copy-start.16
  53.2 3.6 %collective-permute-start.2 = (f32[16,128,128]{2,1,0:T(8,128)S(1)}, f32[16,128,128]{2,1,0:T(8,128)S(1)}, u32[]{:S(2)}, u32[]{:S(2)}) collective-permute-start(f32[16,128,128]{2,1,0:T(8,128)S(1)} %add.77), channel_id=1, source_target_pairs={{0,4},{1,5},{2,6},{3,7},{4,8},{5,9},{6,10},{7,11},{8,12},{9,13},{1... | collective-permute-start | bytes 3145736 | tf_op jit(solution)/shard_map/ppermute | solution.py:14
  56.9 20.8 %collective-permute-done.2 = f32[16,128,128]{2,1,0:T(8,128)S(1)} collective-permute-done((f32[16,128,128]{2,1,0:T(8,128)S(1)}, f32[16,128,128]{2,1,0:T(8,128)S(1)}, u32[]{:S(2)}, u32[]{:S(2)}) %collective-permute-start.2) | collective-permute-done | bytes 1048608 | tf_op jit(solution)/shard_map/ppermute | solution.py:14
  77.6 1.1 add.78
  78.8 1.4 collective-permute-start.3
  80.2 3.1 %fusion.5 = (bf16[384,2048]{1,0:T(8,128)(2,1)}, f32[384,2048]{1,0:T(8,128)}) fusion(bf16[384,2048]{1,0:T(8,128)(2,1)S(1)} %copy-done.16), kind=kLoop, calls=%fused_computation.13 | loop fusion | flops 5505024 | bytes 6291456 | tf_op jit(solution)/shard_map/convert.1
  83.3 2.1 copy.9
  85.4 1.9 copy.37
  87.3 3.1 %select_convert_fusion.1 = bf16[16,384,384]{2,1,0:T(8,128)(2,1)S(1)} fusion(pred[384,384]{1,0:T(8,128)(4,1)S(1)} %iota_compare_fusion, bf16[384,16,128]{0,2,1:T(8,128)(2,1)S(1)} %bitcast.77, bf16[48,16,8,128]{3,2,1,0:T(8,128)(2,1)} %get-tuple-element.11), kind=kOutput, calls=%fused_computation.1 | convolution fusion | flops 608698368 | bytes 8011776 | tf_op jit(solution)/shard_map/thd,shd->hts/dot_general | solution.py:41
  90.4 1.6 fusion.10
  92.1 0.5 copy-done.4
  92.6 11.0 %collective-permute-done.3 = f32[16,128,128]{2,1,0:T(8,128)} collective-permute-done((f32[16,128,128]{2,1,0:T(8,128)}, f32[16,128,128]{2,1,0:T(8,128)}, u32[]{:S(2)}, u32[]{:S(2)}) %collective-permute-start.3) | collective-permute-done | bytes 1048608 | tf_op jit(solution)/shard_map/ppermute | solution.py:14
  103.5 1.8 subtract_convert_fusion.1
  105.3 0.0 copy-start.18
  105.3 0.7 multiply_reduce_fusion.2
  106.1 0.0 copy-done.13
  106.1 1.3 copy-done.1
  107.4 1.3 multiply_reduce_fusion
  108.7 0.8 divide_convert_fusion
  109.5 0.0 copy-start.2
  109.5 0.8 fusion.28
  110.3 23.0 %collective-permute-start.4 = (f32[16,128,128]{2,1,0:T(8,128)S(1)}, f32[16,128,128]{2,1,0:T(8,128)S(1)}, u32[]{:S(2)}, u32[]{:S(2)}) collective-permute-start(f32[16,128,128]{2,1,0:T(8,128)S(1)} %fusion.28), channel_id=1, source_target_pairs={{1,0},{2,1},{3,2},{4,3},{5,4},{6,5},{7,6},{8,7},{9,8},{10,9},{11,1... | collective-permute-start | bytes 3145736 | tf_op jit(solution)/shard_map/ppermute | solution.py:14
  133.3 12.3 %collective-permute-done.4 = f32[16,128,128]{2,1,0:T(8,128)S(1)} collective-permute-done((f32[16,128,128]{2,1,0:T(8,128)S(1)}, f32[16,128,128]{2,1,0:T(8,128)S(1)}, u32[]{:S(2)}, u32[]{:S(2)}) %collective-permute-start.4) | collective-permute-done | bytes 1048608 | tf_op jit(solution)/shard_map/ppermute | solution.py:14
  145.6 1.1 add.85
  146.8 4.0 %collective-permute-start.5 = (f32[16,128,128]{2,1,0:T(8,128)}, f32[16,128,128]{2,1,0:T(8,128)}, u32[]{:S(2)}, u32[]{:S(2)}) collective-permute-start(f32[16,128,128]{2,1,0:T(8,128)} %add.85), channel_id=1, source_target_pairs={{2,0},{3,1},{4,2},{5,3},{6,4},{7,5},{8,6},{9,7},{10,8},{11,9},{12,... | collective-permute-start | bytes 3145736 | tf_op jit(solution)/shard_map/ppermute | solution.py:14
  150.8 3.6 %copy.21 = f32[384,2048]{0,1:T(8,128)} copy(f32[384,2048]{1,0:T(8,128)} %get-tuple-element.14) | data formatting | bytes 6291456 | tf_op jit(solution)/shard_map/jit(_where)/select_n | solution.py:22
  154.4 3.7 %copy.26 = f32[384,2048]{0,1:T(8,128)} copy(f32[384,2048]{1,0:T(8,128)} %get-tuple-element.10) | data formatting | bytes 6291456 | tf_op jit(solution)/shard_map/jit(_where)/select_n | solution.py:22
  158.1 16.1 %collective-permute-done.5 = f32[16,128,128]{2,1,0:T(8,128)} collective-permute-done((f32[16,128,128]{2,1,0:T(8,128)}, f32[16,128,128]{2,1,0:T(8,128)}, u32[]{:S(2)}, u32[]{:S(2)}) %collective-permute-start.5) | collective-permute-done | bytes 1048608 | tf_op jit(solution)/shard_map/ppermute | solution.py:14
  174.1 1.7 add.86
  175.8 0.0 copy-start.6
  175.8 2.8 %collective-permute-start.6 = (f32[16,128,128]{2,1,0:T(8,128)S(1)}, f32[16,128,128]{2,1,0:T(8,128)S(1)}, u32[]{:S(2)}, u32[]{:S(2)}) collective-permute-start(f32[16,128,128]{2,1,0:T(8,128)S(1)} %add.86), channel_id=1, source_target_pairs={{4,0},{5,1},{6,2},{7,3},{8,4},{9,5},{10,6},{11,7},{12,8},{13,9},{1... | collective-permute-start | bytes 3145736 | tf_op jit(solution)/shard_map/ppermute | solution.py:14
  178.7 1.7 select_convert_fusion
  180.4 0.5 collective-permute-start.8
  181.0 1.6 fusion.26
  182.5 0.0 collective-permute-done.8
  182.6 2.8 %collective-permute-start.9 = (f32[16,128]{1,0:T(8,128)S(1)}, f32[16,128]{1,0:T(8,128)S(1)}, u32[]{:S(2)}, u32[]{:S(2)}) collective-permute-start(f32[16,128]{1,0:T(8,128)S(1)} %add.92), channel_id=1, source_target_pairs={{0,2},{1,3},{2,0},{3,1},{4,6},{5,7},{6,4},{7,5},{8,10},{9,11},{10,... | collective-permute-start | bytes 24584 | tf_op jit(solution)/shard_map/ppermute | solution.py:63
  185.3 1.9 fusion.9
  187.3 0.7 collective-permute-start.10
  188.0 15.9 %collective-permute-done.6 = f32[16,128,128]{2,1,0:T(8,128)S(1)} collective-permute-done((f32[16,128,128]{2,1,0:T(8,128)S(1)}, f32[16,128,128]{2,1,0:T(8,128)S(1)}, u32[]{:S(2)}, u32[]{:S(2)}) %collective-permute-start.6) | collective-permute-done | bytes 1048608 | tf_op jit(solution)/shard_map/ppermute | solution.py:14
  203.9 1.1 add.87
  205.0 3.0 %collective-permute-start.7 = (f32[16,128,128]{2,1,0:T(8,128)}, f32[16,128,128]{2,1,0:T(8,128)}, u32[]{:S(2)}, u32[]{:S(2)}) collective-permute-start(f32[16,128,128]{2,1,0:T(8,128)} %add.87), channel_id=1, source_target_pairs={{8,0},{9,1},{10,2},{11,3},{12,4},{13,5},{14,6},{15,7},{24,16},{25,... | collective-permute-start | bytes 3145736 | tf_op jit(solution)/shard_map/ppermute | solution.py:14
  208.0 2.9 %fusion.29 = f32[16,128,384]{2,1,0:T(8,128)} fusion(bf16[384,16,128]{0,2,1:T(8,128)(2,1)S(1)} %copy-done.3, bf16[16,384,384]{2,1,0:T(8,128)(2,1)S(1)} %bitcast.82), kind=kOutput, calls=%fused_computation.52 | convolution fusion | flops 603979776 | bytes 9437184 | tf_op jit(solution)/shard_map/hts,the->she/dot_general | solution.py:78
  210.9 2.9 %fusion.27 = f32[16,128,384]{2,1,0:T(8,128)} fusion(bf16[384,16,128]{0,2,1:T(8,128)(2,1)S(1)} %bitcast.80, bf16[16,384,384]{2,1,0:T(8,128)(2,1)S(1)} %select_convert_fusion), kind=kOutput, calls=%fused_computation.50 | convolution fusion | flops 603979776 | bytes 9437184 | tf_op jit(solution)/shard_map/hts,thd->shd/dot_general | solution.py:74
  213.8 2.7 %copy.29 = bf16[384,2048]{1,0:T(8,128)(2,1)} copy(bf16[384,2048]{0,1:T(8,128)(2,1)} %bitcast.85) | data formatting | bytes 3145728
  216.5 36.4 %collective-permute-done.11 = f32[16,128]{1,0:T(8,128)S(1)} collective-permute-done((f32[16,128]{1,0:T(8,128)S(1)}, f32[16,128]{1,0:T(8,128)S(1)}, u32[]{:S(2)}, u32[]{:S(2)}) %collective-permute-start.11) | collective-permute-done | bytes 8224 | tf_op jit(solution)/shard_map/ppermute | solution.py:63
  252.9 0.6 add_bitcast_fusion
  253.5 0.0 collective-permute-done.7
  253.5 1.7 subtract_convert_fusion
  255.2 2.4 add_convert_fusion
  257.7 1.6 copy.31
  259.3 3.8 %fusion.8 = bf16[384,16,128]{0,2,1:T(8,128)(2,1)S(1)} fusion(f32[384,16,128]{0,2,1:T(8,128)} %bitcast.83, f32[16,128,384]{2,1,0:T(8,128)} %fusion.27, bf16[16,128,128]{2,1,0:T(8,128)(2,1)} %copy-done.15, bf16[384,2048]{1,0:T(8,128)(2,1)S(1)} %copy-done), kind=kOutput, calls=%fused_computation.17 | convolution fusion | flops 203685888 | bytes 9961472 | tf_op jit(solution)/shard_map/the,hde->thd/dot_general | solution.py:75
  263.1 1.6 copy.30
  (43 shorter events, 0.1 us)
Async XLA Ops:
  0.6 8.6 %copy-start = (bf16[384,2048]{1,0:T(8,128)(2,1)S(1)}, bf16[384,2048]{1,0:T(8,128)(2,1)}, u32[]{:S(2)}) copy-start(bf16[384,2048]{1,0:T(8,128)(2,1)} %param.7) | copy-start | bytes 4718596
  9.2 17.7 %copy-start.5 = (bf16[384,16,128]{0,2,1:T(8,128)(2,1)}, bf16[384,16,128]{0,2,1:T(8,128)(2,1)S(1)}, u32[]{:S(2)}) copy-start(bf16[384,16,128]{0,2,1:T(8,128)(2,1)S(1)} %copy.19) | copy-start | bytes 4718596
  9.8 43.4 %copy-start.11 = (f32[16,128,128]{2,1,0:T(8,128)}, f32[16,128,128]{2,1,0:T(8,128)S(1)}, u32[]{:S(2)}) copy-start(f32[16,128,128]{2,1,0:T(8,128)S(1)} %fusion.14) | copy-start | bytes 3145732
  9.8 17.0 %collective-permute-start = (f32[16,128,128]{2,1,0:T(8,128)S(1)}, f32[16,128,128]{2,1,0:T(8,128)S(1)}, u32[]{:S(2)}, u32[]{:S(2)}) collective-permute-start(f32[16,128,128]{2,1,0:T(8,128)S(1)} %fusion.14), channel_id=1, source_target_pairs={{0,1},{1,2},{2,3},{3,4},{4,5},{5,6},{6,7},{7,8},{8,9},{9,10},{10,1... | collective-permute-start | bytes 3145736 | tf_op jit(solution)/shard_map/ppermute | solution.py:14
  27.0 26.1 %collective-permute-start.1 = (f32[16,128,128]{2,1,0:T(8,128)S(1)}, f32[16,128,128]{2,1,0:T(8,128)S(1)}, u32[]{:S(2)}, u32[]{:S(2)}) collective-permute-start(f32[16,128,128]{2,1,0:T(8,128)S(1)} %add.76), channel_id=1, source_target_pairs={{0,2},{1,3},{2,4},{3,5},{4,6},{5,7},{6,8},{7,9},{8,10},{9,11},{10,... | collective-permute-start | bytes 3145736 | tf_op jit(solution)/shard_map/ppermute | solution.py:14
  53.2 26.9 %copy-start.16 = (bf16[384,2048]{1,0:T(8,128)(2,1)S(1)}, bf16[384,2048]{1,0:T(8,128)(2,1)}, u32[]{:S(2)}) copy-start(bf16[384,2048]{1,0:T(8,128)(2,1)} %param.5) | copy-start | bytes 4718596
  53.2 24.4 %collective-permute-start.2 = (f32[16,128,128]{2,1,0:T(8,128)S(1)}, f32[16,128,128]{2,1,0:T(8,128)S(1)}, u32[]{:S(2)}, u32[]{:S(2)}) collective-permute-start(f32[16,128,128]{2,1,0:T(8,128)S(1)} %add.77), channel_id=1, source_target_pairs={{0,4},{1,5},{2,6},{3,7},{4,8},{5,9},{6,10},{7,11},{8,12},{9,13},{1... | collective-permute-start | bytes 3145736 | tf_op jit(solution)/shard_map/ppermute | solution.py:14
  78.8 4.5 %copy-start.17 = (bf16[384,2048]{1,0:T(8,128)(2,1)S(1)}, bf16[384,2048]{1,0:T(8,128)(2,1)}, u32[]{:S(2)}) copy-start(bf16[384,2048]{1,0:T(8,128)(2,1)} %param.8) | copy-start | bytes 4718596
  78.8 24.8 %collective-permute-start.3 = (f32[16,128,128]{2,1,0:T(8,128)}, f32[16,128,128]{2,1,0:T(8,128)}, u32[]{:S(2)}, u32[]{:S(2)}) collective-permute-start(f32[16,128,128]{2,1,0:T(8,128)} %add.78), channel_id=1, source_target_pairs={{0,8},{1,9},{2,10},{3,11},{4,12},{5,13},{6,14},{7,15},{16,24},{17,... | collective-permute-start | bytes 3145736 | tf_op jit(solution)/shard_map/ppermute | solution.py:14
  90.4 2.2 copy-start.4
  90.4 13.1 %copy-start.12 = (f32[16,128,128]{2,1,0:T(8,128)S(1)}, f32[16,128,128]{2,1,0:T(8,128)}, u32[]{:S(2)}) copy-start(f32[16,128,128]{2,1,0:T(8,128)} %copy-done.11) | copy-start | bytes 3145732
  105.3 0.8 copy-start.13
  105.3 2.1 copy-start.1
  105.3 2.1 copy-start.18
  109.5 37.2 %copy-start.2 = (bf16[384,16,128]{0,2,1:T(8,128)(2,1)}, bf16[384,16,128]{0,2,1:T(8,128)(2,1)S(1)}, u32[]{:S(2)}) copy-start(bf16[384,16,128]{0,2,1:T(8,128)(2,1)S(1)} %divide_convert_fusion) | copy-start | bytes 4718596
  110.3 40.5 %copy-start.9 = (f32[16,128,128]{2,1,0:T(8,128)}, f32[16,128,128]{2,1,0:T(8,128)S(1)}, u32[]{:S(2)}) copy-start(f32[16,128,128]{2,1,0:T(8,128)S(1)} %fusion.28) | copy-start | bytes 3145732
  110.3 35.3 %collective-permute-start.4 = (f32[16,128,128]{2,1,0:T(8,128)S(1)}, f32[16,128,128]{2,1,0:T(8,128)S(1)}, u32[]{:S(2)}, u32[]{:S(2)}) collective-permute-start(f32[16,128,128]{2,1,0:T(8,128)S(1)} %fusion.28), channel_id=1, source_target_pairs={{1,0},{2,1},{3,2},{4,3},{5,4},{6,5},{7,6},{8,7},{9,8},{10,9},{11,1... | collective-permute-start | bytes 3145736 | tf_op jit(solution)/shard_map/ppermute | solution.py:14
  146.8 27.4 %collective-permute-start.5 = (f32[16,128,128]{2,1,0:T(8,128)}, f32[16,128,128]{2,1,0:T(8,128)}, u32[]{:S(2)}, u32[]{:S(2)}) collective-permute-start(f32[16,128,128]{2,1,0:T(8,128)} %add.85), channel_id=1, source_target_pairs={{2,0},{3,1},{4,2},{5,3},{6,4},{7,5},{8,6},{9,7},{10,8},{11,9},{12,... | collective-permute-start | bytes 3145736 | tf_op jit(solution)/shard_map/ppermute | solution.py:14
  158.1 20.6 %copy-start.3 = (bf16[384,16,128]{0,2,1:T(8,128)(2,1)S(1)}, bf16[384,16,128]{0,2,1:T(8,128)(2,1)}, u32[]{:S(2)}) copy-start(bf16[384,16,128]{0,2,1:T(8,128)(2,1)} %copy-done.2) | copy-start | bytes 4718596
  175.8 5.1 %copy-start.6 = (bf16[384,16,128]{0,2,1:T(8,128)(2,1)S(1)}, bf16[384,16,128]{0,2,1:T(8,128)(2,1)}, u32[]{:S(2)}) copy-start(bf16[384,16,128]{0,2,1:T(8,128)(2,1)} %copy-done.5) | copy-start | bytes 4718596
  175.8 28.1 %collective-permute-start.6 = (f32[16,128,128]{2,1,0:T(8,128)S(1)}, f32[16,128,128]{2,1,0:T(8,128)S(1)}, u32[]{:S(2)}, u32[]{:S(2)}) collective-permute-start(f32[16,128,128]{2,1,0:T(8,128)S(1)} %add.86), channel_id=1, source_target_pairs={{4,0},{5,1},{6,2},{7,3},{8,4},{9,5},{10,6},{11,7},{12,8},{13,9},{1... | collective-permute-start | bytes 3145736 | tf_op jit(solution)/shard_map/ppermute | solution.py:14
  180.4 4.9 %copy-start.7 = (f32[384,2048]{0,1:T(8,128)S(1)}, f32[384,2048]{0,1:T(8,128)}, u32[]{:S(2)}) copy-start(f32[384,2048]{0,1:T(8,128)} %copy.21) | copy-start | bytes 9437188
  180.4 4.9 %copy-start.14 = (bf16[16,128,128]{2,1,0:T(8,128)(2,1)S(1)}, bf16[16,128,128]{2,1,0:T(8,128)(2,1)}, u32[]{:S(2)}) copy-start(bf16[16,128,128]{2,1,0:T(8,128)(2,1)} %copy-done.13) | copy-start | bytes 1572868
  180.4 2.1 collective-permute-start.8
  182.6 4.7 %collective-permute-start.9 = (f32[16,128]{1,0:T(8,128)S(1)}, f32[16,128]{1,0:T(8,128)S(1)}, u32[]{:S(2)}, u32[]{:S(2)}) collective-permute-start(f32[16,128]{1,0:T(8,128)S(1)} %add.92), channel_id=1, source_target_pairs={{0,2},{1,3},{2,0},{3,1},{4,6},{5,7},{6,4},{7,5},{8,10},{9,11},{10,... | collective-permute-start | bytes 24584 | tf_op jit(solution)/shard_map/ppermute | solution.py:63
  185.3 22.7 %slice-start = ((s8[4718592]{0:T(1024)(128)(4,1)}), s8[4194304]{0:T(1024)(128)(4,1)S(1)}, s32[]{:S(2)}) async-start(s8[4718592]{0:T(1024)(128)(4,1)} %bitcast.81), calls=%async_computation | async-start | bytes 8388608
  185.3 22.7 %slice-start.1 = ((s8[4718592]{0:T(1024)(128)(4,1)}), s8[524288]{0:T(1024)(128)(4,1)S(1)}, s32[]{:S(2)}) async-start(s8[4718592]{0:T(1024)(128)(4,1)} %bitcast.81), calls=%async_computation.1 | async-start | bytes 1048576
  187.3 23.6 %collective-permute-start.10 = (f32[16,128]{1,0:T(8,128)S(1)}, f32[16,128]{1,0:T(8,128)S(1)}, u32[]{:S(2)}, u32[]{:S(2)}) collective-permute-start(f32[16,128]{1,0:T(8,128)S(1)} %add.93), channel_id=1, source_target_pairs={{0,4},{1,5},{2,6},{3,7},{4,0},{5,1},{6,2},{7,3},{8,12},{9,13},{10,... | collective-permute-start | bytes 24584 | tf_op jit(solution)/shard_map/ppermute | solution.py:63
  205.0 48.5 %collective-permute-start.7 = (f32[16,128,128]{2,1,0:T(8,128)}, f32[16,128,128]{2,1,0:T(8,128)}, u32[]{:S(2)}, u32[]{:S(2)}) collective-permute-start(f32[16,128,128]{2,1,0:T(8,128)} %add.87), channel_id=1, source_target_pairs={{8,0},{9,1},{10,2},{11,3},{12,4},{13,5},{14,6},{15,7},{24,16},{25,... | collective-permute-start | bytes 3145736 | tf_op jit(solution)/shard_map/ppermute | solution.py:14
  210.9 42.0 %collective-permute-start.11 = (f32[16,128]{1,0:T(8,128)S(1)}, f32[16,128]{1,0:T(8,128)S(1)}, u32[]{:S(2)}, u32[]{:S(2)}) collective-permute-start(f32[16,128]{1,0:T(8,128)S(1)} %add.94), channel_id=1, source_target_pairs={{0,8},{1,9},{2,10},{3,11},{4,12},{5,13},{6,14},{7,15},{8,0},{9,1},... | collective-permute-start | bytes 24584 | tf_op jit(solution)/shard_map/ppermute | solution.py:63
  213.8 39.7 %copy-start.10 = (f32[16,128,128]{2,1,0:T(8,128)S(1)}, f32[16,128,128]{2,1,0:T(8,128)}, u32[]{:S(2)}) copy-start(f32[16,128,128]{2,1,0:T(8,128)} %copy-done.9) | copy-start | bytes 3145732
  216.5 38.8 %copy-start.8 = (f32[16,128,384]{2,1,0:T(8,128)S(1)}, f32[16,128,384]{2,1,0:T(8,128)}, u32[]{:S(2)}) copy-start(f32[16,128,384]{2,1,0:T(8,128)} %fusion.29) | copy-start | bytes 9437188
  255.2 2.4 copy-start.15
